TPU v7x, 256 devices: a whole 4x4x8 slice. The times are simulated.
256 devices in a mesh: row: 8 (over z_lo, core), col: 16 (over y, x), samp: 2 (over z_hi).
Axes of the slice: x: 4, y: 4, z: 8 (z_hi: 2, z_lo: 4; z = z_hi * 4 + z_lo), core: 2. Of those that a mesh axis runs over, the one named last changes fastest.
Arguments:
- pair_in: bfloat16 [512, 512, 128], P('row', 'col'), may hold values from -6 to 6
- residue_index: int32 [512], replicated, may hold values from 0 to 47
- chain_index: int32 [512], replicated, may hold values from 0 to 2
- token_mask: int32 [512], replicated, may hold values 0 or 1
- relpos_weight: bfloat16 [66, 128], replicated, may hold values from -5 to 5
- tri_proj: bfloat16 [128, 640], replicated, may hold values from -0.5 to 0.5
- tri_out: bfloat16 [128, 128], replicated, may hold values from -0.5 to 0.5
- bias_proj: bfloat16 [128, 16], replicated, may hold values from -0.5 to 0.5
- single: bfloat16 [512, 384], P('row'), may hold values from -6 to 6
- ada_proj: bfloat16 [384, 2304], replicated, may hold values from -0.3125 to 0.3125
- noisy: bfloat16 [16, 512, 768], P('samp', 'row'), may hold values from -6 to 6
- qkv_proj: bfloat16 [768, 3, 768], P(None, None, 'col'), may hold values from -0.21875 to 0.21875
- out_proj: bfloat16 [768, 768], P('col'), may hold values from -0.21875 to 0.21875
- cotangent: bfloat16 [16, 512, 768], P('samp', 'row', 'col'), may hold values from -6 to 6
Outputs:
- pair_out: bfloat16 [512, 512, 128], P('row', 'col')
- block_out: bfloat16 [16, 512, 768], P('samp', 'row', 'col')
- grad_pair: float32 [512, 512, 128], P('row', 'col')
- grad_single: float32 [512, 384], P('row')
All inputs are finite; a program needn't handle non-finite values.
Results may differ from a plain program's by a relative error of at most 0.012.
The roundings to bfloat16 on the way count: a program that leaves them out, or rounds other values in their place, can miss the bound.
Values may be sent and summed in bfloat16 or wider, within the bound.
A program may use at most 128 MiB of HBM per device.

v0:
```python
import jax
import jax.numpy as jnp
from jax import lax
from jax.sharding import PartitionSpec as P

HEAD_DIM = 48
REL_BINS = 66
EPSILON = 1e-05
HIGHEST = lax.Precision.HIGHEST


def joined_along(blocks, dim):
    dims = list(blocks.shape[1:])
    dims[dim] *= blocks.shape[0]
    return jnp.moveaxis(blocks, 0, dim).reshape(dims)


def sent_to_all(array, axis):
    copies = jnp.broadcast_to(array, (lax.axis_size(axis), *array.shape))
    return lax.all_to_all(copies, axis, split_axis=0, concat_axis=0, tiled=True)


def collect(array, axis, dim):
    return joined_along(sent_to_all(array, axis), dim)


def split_up(array, dim, size):
    dims = array.shape
    blocks = array.reshape(*dims[:dim], size, dims[dim] // size, *dims[dim + 1 :])
    return jnp.moveaxis(blocks, dim, 0)


def sent_and_summed(array, axis, dim):
    size = lax.axis_size(axis)
    blocks = lax.all_to_all(split_up(array, dim, size), axis, 0, 0, tiled=True)
    return jnp.sum(blocks, axis=0)


def gathered_total(array, axis):
    return lax.all_gather(array, axis).sum(0)


def taken_together(array, axis):
    return sent_to_all(array, axis).sum(axis=0)


def normalize(values_in):
    average = jnp.mean(values_in, -1, keepdims=True)
    centered = values_in - average
    variance = jnp.mean(centered * centered, -1, keepdims=True)
    return centered * lax.rsqrt(variance + EPSILON)


def normalize_grad(values_in, upstream):
    average = jnp.mean(values_in, -1, keepdims=True)
    centered = values_in - average
    variance = jnp.mean(centered * centered, -1, keepdims=True)
    inv_std = lax.rsqrt(variance + EPSILON)
    unit_rows = centered * inv_std
    return inv_std * (
        upstream
        - jnp.mean(upstream, -1, keepdims=True)
        - unit_rows * jnp.mean(upstream * unit_rows, -1, keepdims=True)
    )


def relative_embedding(res_rows, res_cols, chain_rows, chain_cols, relpos_weight):
    max_offset = (REL_BINS - 2) // 2
    offset = res_rows[:, None] - res_cols[None, :]
    bucket = jnp.where(
        chain_rows[:, None] == chain_cols[None, :],
        jnp.clip(offset + max_offset, 0, 2 * max_offset),
        REL_BINS - 1,
    )
    onehot = (bucket[:, :, None] == jnp.arange(REL_BINS, dtype=jnp.int32)[None, None, :]).astype(
        jnp.bfloat16
    )
    return jnp.einsum("ijr,rc->ijc", onehot, relpos_weight, preferred_element_type=jnp.float32)


def on_device(
    pair_in,
    residue_index,
    chain_index,
    token_mask,
    relpos_weight,
    tri_proj,
    tri_out,
    bias_proj,
    single,
    ada_proj,
    noisy,
    qkv_proj,
    out_proj,
    cotangent,
):
    tile_rows, tile_cols, pair_width = pair_in.shape
    row_at = lax.axis_index("row") * tile_rows
    col_at = lax.axis_index("col") * tile_cols
    res_rows = lax.dynamic_slice_in_dim(residue_index, row_at, tile_rows)
    res_cols = lax.dynamic_slice_in_dim(residue_index, col_at, tile_cols)
    chain_rows = lax.dynamic_slice_in_dim(chain_index, row_at, tile_rows)
    chain_cols = lax.dynamic_slice_in_dim(chain_index, col_at, tile_cols)
    pair_full = pair_in.astype(jnp.float32) + relative_embedding(
        res_rows, res_cols, chain_rows, chain_cols, relpos_weight
    )
    normed_pair = normalize(pair_full).astype(jnp.bfloat16)
    projected = jnp.dot(normed_pair, tri_proj, preferred_element_type=jnp.float32)
    mask_f = token_mask.astype(jnp.float32)
    mask_rows = lax.dynamic_slice_in_dim(mask_f, row_at, tile_rows)
    mask_cols = lax.dynamic_slice_in_dim(mask_f, col_at, tile_cols)
    pair_mask = (mask_rows[:, None] * mask_cols[None, :])[:, :, None]
    left_side = (
        jax.nn.sigmoid(projected[..., pair_width : 2 * pair_width])
        * projected[..., :pair_width]
        * pair_mask
    ).astype(jnp.bfloat16)
    right_side = (
        jax.nn.sigmoid(projected[..., 3 * pair_width : 4 * pair_width])
        * projected[..., 2 * pair_width : 3 * pair_width]
        * pair_mask
    ).astype(jnp.bfloat16)
    tri_gate = jax.nn.sigmoid(projected[..., 4 * pair_width :])
    right_all = lax.all_gather(right_side, "row", axis=0, tiled=True)
    triangle = jnp.swapaxes(
        lax.psum_scatter(
            jnp.einsum("jkc,ikc->jic", right_all, left_side, preferred_element_type=jnp.float32),
            "col",
            scatter_dimension=0,
            tiled=True,
        ),
        0,
        1,
    )
    update = jnp.dot(
        normalize(triangle).astype(jnp.bfloat16), tri_out, preferred_element_type=jnp.float32
    )
    pair_out = (pair_full + tri_gate * update).astype(jnp.bfloat16)
    head_count = qkv_proj.shape[2] // HEAD_DIM
    tile_bias = jnp.einsum(
        "ijc,ch->hij", pair_out, bias_proj, preferred_element_type=jnp.float32
    ).astype(jnp.bfloat16)
    head_bias = lax.all_to_all(tile_bias, "col", split_axis=0, concat_axis=2, tiled=True)
    model_width = noisy.shape[2]
    sample_count, tokens_here = (noisy.shape[0], noisy.shape[1])
    inner_width = qkv_proj.shape[2]
    cvec = normalize(single.astype(jnp.float32)).astype(jnp.bfloat16)
    conditioning = jnp.dot(cvec, ada_proj, preferred_element_type=jnp.float32)
    ada_scale = jax.nn.sigmoid(conditioning[:, :model_width])
    ada_shift = conditioning[:, model_width : 2 * model_width]
    out_gate = jax.nn.sigmoid(conditioning[:, 2 * model_width :])
    normed_in = normalize(noisy.astype(jnp.float32))
    hidden = (ada_scale * normed_in + ada_shift).astype(jnp.bfloat16)
    qkv_all = jnp.einsum(
        "std,dqe->stqe", hidden, qkv_proj, preferred_element_type=jnp.float32
    ).astype(jnp.bfloat16)
    keyval = collect(qkv_all[:, :, 1:], "row", 1)
    key_count = keyval.shape[1]
    queries = qkv_all[:, :, 0].reshape(sample_count, tokens_here, head_count, HEAD_DIM)
    key_rows = keyval[:, :, 0].reshape(sample_count, key_count, head_count, HEAD_DIM)
    value_rows = keyval[:, :, 1].reshape(sample_count, key_count, head_count, HEAD_DIM)
    score_scale = 1.0 / HEAD_DIM**0.5
    key_ok = token_mask > 0
    scores = (
        jnp.einsum("sihd,sjhd->shij", queries, key_rows, preferred_element_type=jnp.float32)
        * score_scale
    )
    scores = scores + head_bias.astype(jnp.float32)[None]
    scores = jnp.where(key_ok[None, None, None, :], scores, -1000000000.0)
    probs = jax.nn.softmax(scores, axis=-1)
    probs_b = probs.astype(jnp.bfloat16)
    attended = jnp.einsum(
        "shij,sjhd->sihd", probs_b, value_rows, preferred_element_type=jnp.float32
    ).astype(jnp.bfloat16)
    attended = attended.reshape(sample_count, tokens_here, inner_width)
    mixed_part = jnp.einsum("ste,ed->std", attended, out_proj, preferred_element_type=jnp.float32)
    mixed = sent_and_summed(mixed_part, "col", 2)
    feature_block = mixed.shape[2]
    feat_at = lax.axis_index("col") * feature_block
    gate_block = lax.dynamic_slice_in_dim(out_gate, feat_at, feature_block, 1)
    noisy_block = lax.dynamic_slice_in_dim(noisy, feat_at, feature_block, 2)
    block_out = (noisy_block.astype(jnp.float32) + gate_block * mixed).astype(jnp.bfloat16)
    grad_in = cotangent.astype(jnp.float32)
    d_mixed = (grad_in * gate_block).astype(jnp.bfloat16)
    d_gate = jnp.sum(grad_in * mixed, 0) * gate_block * (1.0 - gate_block)
    d_att = jnp.einsum(
        "std,ed->ste", collect(d_mixed, "col", 2), out_proj, preferred_element_type=jnp.float32
    )
    d_att = d_att.astype(jnp.bfloat16).reshape(sample_count, tokens_here, head_count, HEAD_DIM)
    d_probs = jnp.einsum("sihd,sjhd->shij", d_att, value_rows, preferred_element_type=jnp.float32)
    d_scores = probs * (d_probs - jnp.sum(probs * d_probs, -1, keepdims=True))
    d_scaled = (d_scores * score_scale).astype(jnp.bfloat16)
    d_query = jnp.einsum(
        "shij,sjhd->sihd", d_scaled, key_rows, preferred_element_type=jnp.float32
    ).astype(jnp.bfloat16)
    d_keys = jnp.einsum("shij,sihd->sjhd", d_scaled, queries, preferred_element_type=jnp.float32)
    d_values = jnp.einsum("shij,sihd->sjhd", probs_b, d_att, preferred_element_type=jnp.float32)
    d_keyval = jnp.stack(
        [
            d_keys.reshape(sample_count, key_count, inner_width),
            d_values.reshape(sample_count, key_count, inner_width),
        ],
        2,
    )
    d_keyval = sent_and_summed(d_keyval, "row", 1).astype(jnp.bfloat16)
    d_qkv = jnp.concatenate([d_query, d_keyval], 2)
    d_hidden = jnp.einsum("stqe,dqe->std", d_qkv, qkv_proj, preferred_element_type=jnp.float32)
    d_scale = jnp.sum(d_hidden * normed_in, 0)
    d_shift = jnp.sum(d_hidden, 0)
    w_ada = ada_proj.astype(jnp.float32)
    w_gate = lax.dynamic_slice_in_dim(w_ada, 2 * model_width + feat_at, feature_block, 1)
    d_cvec = jnp.dot(
        d_scale * ada_scale * (1.0 - ada_scale), w_ada[:, :model_width].T, precision=HIGHEST
    )
    d_cvec = d_cvec + jnp.dot(d_shift, w_ada[:, model_width : 2 * model_width].T, precision=HIGHEST)
    d_cvec = d_cvec + jnp.dot(d_gate, w_gate.T, precision=HIGHEST)
    d_cvec = gathered_total(d_cvec, ("col", "samp"))
    grad_single = normalize_grad(single.astype(jnp.float32), d_cvec)
    d_bias = jnp.sum(d_scores, 0)
    d_bias = taken_together(d_bias, "samp")
    d_tile = lax.all_to_all(d_bias, "col", split_axis=2, concat_axis=0, tiled=True)
    grad_pair = jnp.einsum("hij,ch->ijc", d_tile, bias_proj.astype(jnp.float32), precision=HIGHEST)
    return (pair_out, block_out, grad_pair, grad_single)


def solution(mesh):
    return jax.shard_map(
        on_device,
        mesh=mesh,
        in_specs=(
            P("row", "col", None),
            P(),
            P(),
            P(),
            P(),
            P(),
            P(),
            P(),
            P("row", None),
            P(),
            P("samp", "row", None),
            P(None, None, "col"),
            P("col", None),
            P("samp", "row", "col"),
        ),
        out_specs=(
            P("row", "col", None),
            P("samp", "row", "col"),
            P("row", "col", None),
            P("row", None),
        ),
        check_vma=False,
    )
```

profile of v0, /device:TPU:32, one launch (start us, length us, event | category | flops | bytes accessed | tf_op | source)
XLA Modules:
  0.0 503.7 jit_solution(2397835421734303942)
XLA Ops:
  11.2 1.8 fusion.118
  15.2 1.8 fusion.22
  17.7 1.7 copy.132
  19.5 51.6 %all-gather.4.cloned.1.call-done = bf16[512,32,128]{2,1,0:T(8,128)(2,1)} async-done(((bf16[64,32,128]{2,1,0:T(8,128)(2,1)}), bf16[512,32,128]{2,1,0:T(8,128)(2,1)}) %all-gather.4.cloned.1.call-update) | async-done | bytes 4194320 | tf_op jit(solution)/shard_map/all_gather | solution.py:124
  71.0 8.6 %copy.133 = bf16[512,32,128]{0,1,2:T(8,128)(2,1)} copy(bf16[512,32,128]{2,1,0:T(8,128)(2,1)} %all-gather.4.cloned.1.call-done) | data formatting | bytes 8388608 | tf_op jit(solution)/shard_map/all_gather | solution.py:124
  79.7 10.3 %convolution_bitcast_fusion = f32[512,64,128]{0,1,2:T(8,128)} fusion(bf16[64,32,128]{0,1,2:T(8,128)(2,1)S(1)} %copy.132, bf16[512,32,128]{0,1,2:T(8,128)(2,1)} %copy.133), kind=kOutput, calls=%fused_computation.2 | convolution fusion | flops 268435456 | bytes 21495808 | tf_op jit(solution)/shard_map/jkc,ikc->jic/dot_general | solution.py:127
  89.9 16.8 %copy.134 = f32[512,64,128]{2,1,0:T(8,128)} copy(f32[512,64,128]{0,1,2:T(8,128)} %convolution_bitcast_fusion) | data formatting | bytes 33554432 | tf_op jit(solution)/shard_map/jkc,ikc->jic/transpose | solution.py:127
  108.5 2.0 fusion.82
  113.8 2.0 reshape.267
  115.8 9.1 %all-to-all-start = ((bf16[8,2,24576]{2,1,0:T(2,128)(2,1)}), bf16[8,2,24576]{2,1,0:T(2,128)(2,1)}, u32[]{:S(2)}, u32[]{:S(2)}) async-start(bf16[8,2,24576]{2,1,0:T(2,128)(2,1)} %reshape.267), calls=%async_computation.1 | async-start | bytes 1572864 | tf_op jit(solution)/shard_map/all_to_all | solution.py:20
  125.1 17.2 %all-to-all-done = bf16[8,2,24576]{2,1,0:T(2,128)(2,1)} async-done(((bf16[8,2,24576]{2,1,0:T(2,128)(2,1)}), bf16[8,2,24576]{2,1,0:T(2,128)(2,1)}, u32[]{:S(2)}, u32[]{:S(2)}) %all-to-all-start) | async-done | bytes 786464 | tf_op jit(solution)/shard_map/all_to_all | solution.py:20
  142.4 2.2 reshape.268
  144.6 80.7 %reduce-scatter.2.cloned.1.call-done = f32[32,64,128]{2,1,0:T(8,128)} async-done(((f32[512,64,128]{2,1,0:T(8,128)}), f32[32,64,128]{2,1,0:T(8,128)}) %reduce-scatter.2.cloned.1.call-update) | async-done | bytes 1048592 | tf_op jit(solution)/shard_map/reduce_scatter | solution.py:126
  225.3 1.7 bitcast_reduce_fusion.1
  228.3 1.8 fusion.17
  232.8 4.8 all-to-all-start.1
  239.7 5.5 %all-to-all-done.1 = bf16[16,2,1024]{2,1,0:T(2,128)(2,1)S(1)} async-done(((bf16[16,2,1024]{2,1,0:T(2,128)(2,1)}), bf16[16,2,1024]{2,1,0:T(2,128)(2,1)S(1)}, u32[]{:S(2)}, u32[]{:S(2)}) %all-to-all-start.1) | async-done | bytes 65568 | tf_op jit(solution)/shard_map/all_to_all | solution.py:143
  245.6 1.5 fusion.119
  248.1 2.5 convolution_bitcast_fusion.1
  250.6 2.2 copy.172
  252.8 2.9 reshape.271
  255.7 3.9 all-to-all-start.2
  262.4 19.4 %all-to-all-done.2 = f32[16,1,24576]{2,1,0:T(1,128)S(1)} async-done(((f32[16,1,24576]{2,1,0:T(1,128)}), f32[16,1,24576]{2,1,0:T(1,128)S(1)}, u32[]{:S(2)}, u32[]{:S(2)}) %all-to-all-start.2) | async-done | bytes 1572896 | tf_op jit(solution)/shard_map/all_to_all | solution.py:35
  282.3 6.2 %reduce.12 = f32[16,24576]{1,0:T(8,128)} reduce(f32[16,1,24576]{2,1,0:T(1,128)S(1)} %all-to-all-done.2, f32[]{:T(128)} %broadcast.247), dimensions={1}, to_apply=%all_to_all.37.reduce_sub_computation | reduce | bytes 3145732 | tf_op jit(solution)/shard_map/all_to_all | solution.py:35
  288.5 2.4 reshape.272
  291.8 1.3 fusion.62
  294.7 16.6 %all_to_all.52 = bf16[16,2,12288]{2,1,0:T(2,128)(2,1)S(1)} all-to-all(bf16[16,2,12288]{2,1,0:T(2,128)(2,1)S(1)} %reshape.273), channel_id=1, replica_groups=mesh['row'=8,'col'=16,'samp'=2] {'col'}, dimensions={0} | all-to-all | bytes 1572864 | tf_op jit(solution)/shard_map/all_to_all | solution.py:20
  313.5 3.5 copy.144
  317.1 2.5 reshape.251
  320.1 1.3 fusion.51
  322.4 4.4 convolution_bitcast_fusion.3
  326.8 2.6 pad_maximum_fusion
  329.3 2.4 reshape.252
  331.8 2.2 copy.171
  334.0 4.8 reshape.277
  338.8 5.5 %all-to-all-start.6 = ((f32[8,1,49152]{2,1,0:T(1,128)}), f32[8,1,49152]{2,1,0:T(1,128)S(1)}, u32[]{:S(2)}, u32[]{:S(2)}) async-start(f32[8,1,49152]{2,1,0:T(1,128)} %reshape.277), calls=%async_computation.7 | async-start | bytes 3145728 | tf_op jit(solution)/shard_map/all_to_all | solution.py:35
  344.6 5.4 %fusion.20 = bf16[8,64,1,48]{1,3,2,0:T(8,128)(2,1)} fusion(bf16[8,512,2,48]{1,3,0,2:T(8,128)(2,1)S(1)} %copy-done.8, f32[8,64,512]{2,1,0:T(8,128)} %copy-done.11, f32[8,64,512]{2,1,0:T(8,128)} %copy-done.13, f32[8,64]{1,0:T(8,128)S(1)} %copy-done.33), kind=kOutput, calls=%fused_computation.37 | convolution fusion | flops 27026432 | bytes 4644864 | tf_op jit(solution)/shard_map/shij,sjhd->sihd/dot_general | solution.py:193
  350.1 28.6 %all-to-all-done.6 = f32[8,1,49152]{2,1,0:T(1,128)S(1)} async-done(((f32[8,1,49152]{2,1,0:T(1,128)}), f32[8,1,49152]{2,1,0:T(1,128)S(1)}, u32[]{:S(2)}, u32[]{:S(2)}) %all-to-all-start.6) | async-done | bytes 1572896 | tf_op jit(solution)/shard_map/all_to_all | solution.py:35
  378.7 6.3 %reduce.15 = f32[8,49152]{1,0:T(8,128)} reduce(f32[8,1,49152]{2,1,0:T(1,128)S(1)} %all-to-all-done.6, f32[]{:T(128)} %broadcast.247), dimensions={1}, to_apply=%all_to_all.44.reduce_sub_computation | reduce | bytes 3145732 | tf_op jit(solution)/shard_map/all_to_all | solution.py:35
  384.9 2.7 reshape.278
  390.2 1.6 fusion.42
  393.5 2.8 fusion.120
  396.3 14.8 %all_to_all.53 = f32[2,1,64,512]{3,2,1,0:T(8,128)S(1)} all-to-all(f32[2,1,64,512]{3,2,1,0:T(8,128)S(1)} %broadcast_in_dim.23), channel_id=1, replica_groups=mesh['row'=8,'col'=16,'samp'=2] {'samp'}, dimensions={0} | all-to-all | bytes 524288 | tf_op jit(solution)/shard_map/all_to_all | solution.py:20
  411.3 1.3 reduce.13
  412.8 11.2 %all_to_all.54 = f32[16,1,2048]{2,1,0:T(1,128)S(1)} all-to-all(f32[16,1,2048]{2,1,0:T(1,128)S(1)} %reshape.275), channel_id=1, replica_groups=mesh['row'=8,'col'=16,'samp'=2] {'col'}, dimensions={0} | all-to-all | bytes 262144 | tf_op jit(solution)/shard_map/all_to_all | solution.py:221
  425.7 2.0 fusion.45
  427.7 65.2 %all-gather.6.cloned.1.call-done = f32[2048,384]{1,0:T(8,128)} async-done(((f32[64,384]{1,0:T(8,128)}), f32[2048,384]{1,0:T(8,128)}) %all-gather.6.cloned.1.call-update) | async-done | bytes 3145744 | tf_op jit(solution)/shard_map/all_gather | solution.py:40
  492.9 2.2 reduce_sum.208
  (152 shorter events, 37.0 us)
Async XLA Ops:
  7.2 104.9 %copy-start = (bf16[768,3,48]{0,2,1:T(8,128)(2,1)S(1)}, bf16[768,3,48]{0,2,1:T(8,128)(2,1)}, u32[]{:S(2)}) copy-start(bf16[768,3,48]{0,2,1:T(8,128)(2,1)} %param.25) | copy-start | bytes 663556
  7.2 6.9 %copy-start.19 = (bf16[128,640]{1,0:T(8,128)(2,1)S(1)}, bf16[128,640]{1,0:T(8,128)(2,1)}, u32[]{:S(2)}) copy-start(bf16[128,640]{1,0:T(8,128)(2,1)} %param.19) | copy-start | bytes 491524
  7.2 63.8 %all-gather.4.cloned.1.call-start = ((), (), s32[]{:S(2)}) async-start(), calls=%async_computation.8 | async-start | bytes 4718592 | tf_op jit(solution)/shard_map/all_gather | solution.py:124
  15.1 2.6 copy-start.1
  17.7 207.6 %reduce-scatter.2.cloned.1.call-start = ((), (), s32[]{:S(2)}) async-start(), calls=%async_computation.9 | async-start | bytes 17825792 | tf_op jit(solution)/shard_map/reduce_scatter | solution.py:126
  106.7 0.8 copy-start.10
  106.7 1.2 copy-start.4
  107.7 2.8 copy-start.25
  108.5 3.6 copy-start.28
  108.5 3.6 copy-start.30
  110.5 0.8 copy-start.9
  112.8 0.7 copy-start.20
  113.8 11.1 %copy-start.17 = (bf16[48,768]{1,0:T(8,128)(2,1)S(1)}, bf16[48,768]{1,0:T(8,128)(2,1)}, u32[]{:S(2)}) copy-start(bf16[48,768]{1,0:T(8,128)(2,1)} %param.26) | copy-start | bytes 221188
  113.8 11.3 %copy-start.27 = (s32[512]{0:T(512)S(1)}, s32[512]{0:T(512)}, u32[]{:S(2)}) copy-start(s32[512]{0:T(512)} %param.17) | copy-start | bytes 6148
  115.8 26.6 %all-to-all-start = ((bf16[8,2,24576]{2,1,0:T(2,128)(2,1)}), bf16[8,2,24576]{2,1,0:T(2,128)(2,1)}, u32[]{:S(2)}, u32[]{:S(2)}) async-start(bf16[8,2,24576]{2,1,0:T(2,128)(2,1)} %reshape.267), calls=%async_computation.1 | async-start | bytes 1572864 | tf_op jit(solution)/shard_map/all_to_all | solution.py:20
  225.3 1.7 copy-start.3
  226.9 1.3 copy-start.34
  228.3 2.7 copy-start.24
  230.1 0.8 copy-start.16
  232.8 12.5 %all-to-all-start.1 = ((bf16[16,2,1024]{2,1,0:T(2,128)(2,1)}), bf16[16,2,1024]{2,1,0:T(2,128)(2,1)S(1)}, u32[]{:S(2)}, u32[]{:S(2)}) async-start(bf16[16,2,1024]{2,1,0:T(2,128)(2,1)} %reshape.269), calls=%async_computation.2 | async-start | bytes 131072 | tf_op jit(solution)/shard_map/all_to_all | solution.py:143
  239.7 7.3 %copy-start.7 = (bf16[8,512,2,48]{1,3,0,2:T(8,128)(2,1)}, bf16[8,512,2,48]{1,3,0,2:T(8,128)(2,1)S(1)}, u32[]{:S(2)}) copy-start(bf16[8,512,2,48]{1,3,0,2:T(8,128)(2,1)S(1)} %reshape.246) | copy-start | bytes 2359300
  247.1 1.0 copy-start.13
  247.1 1.0 copy-start.32
  255.7 26.1 %all-to-all-start.2 = ((f32[16,1,24576]{2,1,0:T(1,128)}), f32[16,1,24576]{2,1,0:T(1,128)S(1)}, u32[]{:S(2)}, u32[]{:S(2)}) async-start(f32[16,1,24576]{2,1,0:T(1,128)} %reshape.271), calls=%async_computation.3 | async-start | bytes 3145728 | tf_op jit(solution)/shard_map/all_to_all | solution.py:35
  290.9 0.7 copy-start.22
  290.9 0.9 copy-start.23
  317.1 2.5 copy-start.18
  319.5 1.9 copy-start.14
  319.6 1.9 copy-start.33
  321.4 1.0 copy-start.11
  338.8 5.7 %copy-start.21 = (f32[64,48]{0,1:T(8,128)S(1)}, f32[64,48]{0,1:T(8,128)}, u32[]{:S(2)}) copy-start(f32[64,48]{0,1:T(8,128)} %get-tuple-element.11) | copy-start | bytes 36868
  338.8 5.8 %copy-start.8 = (bf16[8,512,2,48]{1,3,0,2:T(8,128)(2,1)S(1)}, bf16[8,512,2,48]{1,3,0,2:T(8,128)(2,1)}, u32[]{:S(2)}) copy-start(bf16[8,512,2,48]{1,3,0,2:T(8,128)(2,1)} %copy-done.7) | copy-start | bytes 2359300
  338.8 39.8 %all-to-all-start.6 = ((f32[8,1,49152]{2,1,0:T(1,128)}), f32[8,1,49152]{2,1,0:T(1,128)S(1)}, u32[]{:S(2)}, u32[]{:S(2)}) async-start(f32[8,1,49152]{2,1,0:T(1,128)} %reshape.277), calls=%async_computation.7 | async-start | bytes 3145728 | tf_op jit(solution)/shard_map/all_to_all | solution.py:35
  344.3 148.6 %all-gather.6.cloned.1.call-start = ((), (), s32[]{:S(2)}) async-start(), calls=%async_computation.10 | async-start | bytes 3244032 | tf_op jit(solution)/shard_map/all_gather | solution.py:40
  387.6 1.1 copy-start.5
  387.6 1.1 copy-start.31
  387.6 1.1 copy-start.35
  388.7 1.5 copy-start.6
  389.3 4.2 copy-start.12
  389.3 4.2 copy-start.15
  492.9 2.2 copy-start.26
  492.9 2.2 copy-start.29
  492.9 2.8 copy-start.2
Sparse Core Ops, SparseCore 0:
  17.8 53.1 all-gather.3
  106.9 118.3 reduce-scatter.1
  393.6 99.2 all-gather.5
where the time goes:
time: 513 us; the launch traced here: 504 us
  waiting for transfers between devices  268 us (52%)
  local copies, waits for them, and re-layouts  80 us (16%)
  blocking collectives  42.6 us (8%)
  matrix products  40.2 us (8%)
  other arithmetic  34.2 us (7%)
  starting transfers between devices  23.6 us (5%)
  between operations  14.8 us (3%)
    reduce_scatter x1, waiting for transfers between devices, on_device(): lax.psum_scatter(jnp.einsum('jkc,ikc->jic', right_all, left_side, preferr...  80.7 us
    all_gather x1, waiting for transfers between devices, gathered_total(): return lax.all_gather(array, axis).sum(0)  65.2 us
    all_gather x1, waiting for transfers between devices, on_device(): right_all = lax.all_gather(right_side, 'row', axis=0, tiled=True)  51.6 us
    all_to_all x2, waiting for transfers between devices, sent_and_summed(): blocks = lax.all_to_all(split_up(array, dim, size), axis, 0, 0, tiled=True)  47.9 us
    all_to_all x2, blocking collectives, sent_to_all(): return lax.all_to_all(copies, axis, split_axis=0, concat_axis=0, tiled=True)  31.4 us
    unnamed x87, local copies, waits for them, and re-layouts  29.6 us
    all_to_all x1, waiting for transfers between devices, sent_to_all(): return lax.all_to_all(copies, axis, split_axis=0, concat_axis=0, tiled=True)  17.2 us
    transpose x1, local copies, waits for them, and re-layouts, on_device(): jnp.einsum('jkc,ikc->jic', right_all, left_side, preferred_element_type=j...  16.8 us
  transfers between devices with their start and end apart: 7, of which 7 were waited for; matrix products, arithmetic and copies ran while one was open for 6% of the time, Pallas kernels for 0%

commit v1 on v0

--- a/solution.py
+++ b/solution.py
@@ -121,7 +121,9 @@
         * pair_mask
     ).astype(jnp.bfloat16)
     tri_gate = jax.nn.sigmoid(projected[..., 4 * pair_width :])
-    right_all = lax.all_gather(right_side, "row", axis=0, tiled=True)
+    right_all = jnp.concatenate(
+        lax.all_to_all(jnp.stack([right_side] * lax.axis_size("row")), "row", 0, 0), axis=0
+    )
     triangle = jnp.swapaxes(
         lax.psum_scatter(
             jnp.einsum("jkc,ikc->jic", right_all, left_side, preferred_element_type=jnp.float32),

time: 513 us -> 562 us (1.096)
  waiting for transfers between devices: 268 us -> 308 us
    all_to_all x0 -> x1, waiting for transfers between devices: none -> 88.8 us  [on_device(): lax.all_to_all(jnp.stack([right_side] * lax.axis_size('row')), 'row', 0, 0)]
    all_gather x1 -> x0, waiting for transfers between devices: 51.6 us -> none  [on_device(): right_all = lax.all_gather(right_side, 'row', axis=0, tiled=True)]
    all_gather x1 -> x0, local copies, waits for them, and re-layouts: 8.64 us -> none  [on_device(): right_all = lax.all_gather(right_side, 'row', axis=0, tiled=True)]
    reshape x0 -> x1, local copies, waits for them, and re-layouts: none -> 8.6 us  [on_device(): jnp.concatenate(lax.all_to_all(jnp.stack([right_side] * lax.axis_size('ro...]
    all_to_all x0 -> x1, starting transfers between devices: none -> 6.24 us  [on_device(): lax.all_to_all(jnp.stack([right_side] * lax.axis_size('row')), 'row', 0, 0)]
  transfers between devices with their start and end apart: 7 -> 7, of which waited for: 7 -> 7; matrix products, arithmetic and copies ran while one was open for 6% -> 5% of each run, Pallas kernels for 0% -> 0%
where the time goes in v1:
time: 562 us; the launch traced here: 552 us
  waiting for transfers between devices  308 us (55%)
  local copies, waits for them, and re-layouts  83.7 us (15%)
  blocking collectives  42.7 us (8%)
  matrix products  40.1 us (7%)
  other arithmetic  33 us (6%)
  starting transfers between devices  28.9 us (5%)
  between operations  15.3 us (3%)
    all_to_all x1, waiting for transfers between devices, on_device(): lax.all_to_all(jnp.stack([right_side] * lax.axis_size('row')), 'row', 0, 0)  88.8 us
    reduce_scatter x1, waiting for transfers between devices, on_device(): lax.psum_scatter(jnp.einsum('jkc,ikc->jic', right_all, left_side, preferr...  83.4 us
    all_gather x1, waiting for transfers between devices, gathered_total(): return lax.all_gather(array, axis).sum(0)  65.2 us
    all_to_all x2, waiting for transfers between devices, sent_and_summed(): blocks = lax.all_to_all(split_up(array, dim, size), axis, 0, 0, tiled=True)  48 us
    all_to_all x2, blocking collectives, sent_to_all(): return lax.all_to_all(copies, axis, split_axis=0, concat_axis=0, tiled=True)  31.5 us
    unnamed x87, local copies, waits for them, and re-layouts  30.7 us
    all_to_all x1, waiting for transfers between devices, sent_to_all(): return lax.all_to_all(copies, axis, split_axis=0, concat_axis=0, tiled=True)  17.2 us
    transpose x1, local copies, waits for them, and re-layouts, on_device(): jnp.einsum('jkc,ikc->jic', right_all, left_side, preferred_element_type=j...  16.8 us
  transfers between devices with their start and end apart: 7, of which 7 were waited for; matrix products, arithmetic and copies ran while one was open for 5% of the time, Pallas kernels for 0%

profile of v1, /device:TPU:32, one launch (start us, length us, event | category | flops | bytes accessed | tf_op | source)
XLA Modules:
  0.0 551.9 jit_solution(4047227765900731330)
XLA Ops:
  11.2 1.8 fusion.118
  15.8 1.7 copy-done.1
  17.5 2.7 stack.4
  20.2 6.2 %all-to-all-start = ((bf16[8,64,32,128]{3,2,1,0:T(8,128)(2,1)}), bf16[8,64,32,128]{3,2,1,0:T(8,128)(2,1)}, u32[]{:S(2)}, u32[]{:S(2)}) async-start(bf16[8,64,32,128]{3,2,1,0:T(8,128)(2,1)} %stack.4), calls=%async_computation | async-start | bytes 8388608 | tf_op jit(solution)/shard_map/all_to_all | solution.py:125
  26.4 1.7 copy.132
  28.2 88.8 %all-to-all-done = bf16[8,64,32,128]{3,2,1,0:T(8,128)(2,1)} async-done(((bf16[8,64,32,128]{3,2,1,0:T(8,128)(2,1)}), bf16[8,64,32,128]{3,2,1,0:T(8,128)(2,1)}, u32[]{:S(2)}, u32[]{:S(2)}) %all-to-all-start) | async-done | bytes 4194336 | tf_op jit(solution)/shard_map/all_to_all | solution.py:125
  117.0 8.6 %copy.133 = bf16[512,32,128]{0,1,2:T(8,128)(2,1)} copy(bf16[512,32,128]{2,1,0:T(8,128)(2,1)} %bitcast.2) | data formatting | bytes 8388608 | tf_op jit(solution)/shard_map/reshape | solution.py:124
  125.6 10.3 %convolution_bitcast_fusion = f32[512,64,128]{0,1,2:T(8,128)} fusion(bf16[64,32,128]{0,1,2:T(8,128)(2,1)S(1)} %copy.132, bf16[512,32,128]{0,1,2:T(8,128)(2,1)} %copy.133), kind=kOutput, calls=%fused_computation.2 | convolution fusion | flops 268435456 | bytes 21495808 | tf_op jit(solution)/shard_map/jkc,ikc->jic/dot_general | solution.py:129
  135.8 16.8 %copy.134 = f32[512,64,128]{2,1,0:T(8,128)} copy(f32[512,64,128]{0,1,2:T(8,128)} %convolution_bitcast_fusion) | data formatting | bytes 33554432 | tf_op jit(solution)/shard_map/jkc,ikc->jic/transpose | solution.py:129
  154.4 2.0 fusion.82
  159.7 2.0 reshape.273
  161.7 8.3 %all-to-all-start.1 = ((bf16[8,2,24576]{2,1,0:T(2,128)(2,1)}), bf16[8,2,24576]{2,1,0:T(2,128)(2,1)}, u32[]{:S(2)}, u32[]{:S(2)}) async-start(bf16[8,2,24576]{2,1,0:T(2,128)(2,1)} %reshape.273), calls=%async_computation.2 | async-start | bytes 1572864 | tf_op jit(solution)/shard_map/all_to_all | solution.py:20
  170.1 17.2 %all-to-all-done.1 = bf16[8,2,24576]{2,1,0:T(2,128)(2,1)} async-done(((bf16[8,2,24576]{2,1,0:T(2,128)(2,1)}), bf16[8,2,24576]{2,1,0:T(2,128)(2,1)}, u32[]{:S(2)}, u32[]{:S(2)}) %all-to-all-start.1) | async-done | bytes 786464 | tf_op jit(solution)/shard_map/all_to_all | solution.py:20
  187.4 2.2 reshape.274
  189.6 83.4 %reduce-scatter.2.cloned.1.call-done = f32[32,64,128]{2,1,0:T(8,128)} async-done(((f32[512,64,128]{2,1,0:T(8,128)}), f32[32,64,128]{2,1,0:T(8,128)}) %reduce-scatter.2.cloned.1.call-update) | async-done | bytes 1048592 | tf_op jit(solution)/shard_map/reduce_scatter | solution.py:128
  273.0 1.7 bitcast_reduce_fusion.1
  276.0 1.8 fusion.17
  280.5 4.9 all-to-all-start.2
  287.5 5.5 %all-to-all-done.2 = bf16[16,2,1024]{2,1,0:T(2,128)(2,1)S(1)} async-done(((bf16[16,2,1024]{2,1,0:T(2,128)(2,1)}), bf16[16,2,1024]{2,1,0:T(2,128)(2,1)S(1)}, u32[]{:S(2)}, u32[]{:S(2)}) %all-to-all-start.2) | async-done | bytes 65568 | tf_op jit(solution)/shard_map/all_to_all | solution.py:145
  293.3 1.5 fusion.119
  295.8 2.5 convolution_bitcast_fusion.1
  298.3 2.2 copy.172
  300.5 2.9 reshape.277
  303.4 3.9 all-to-all-start.3
  310.1 19.4 %all-to-all-done.3 = f32[16,1,24576]{2,1,0:T(1,128)S(1)} async-done(((f32[16,1,24576]{2,1,0:T(1,128)}), f32[16,1,24576]{2,1,0:T(1,128)S(1)}, u32[]{:S(2)}, u32[]{:S(2)}) %all-to-all-start.3) | async-done | bytes 1572896 | tf_op jit(solution)/shard_map/all_to_all | solution.py:35
  330.1 6.2 %reduce.12 = f32[16,24576]{1,0:T(8,128)} reduce(f32[16,1,24576]{2,1,0:T(1,128)S(1)} %all-to-all-done.3, f32[]{:T(128)} %broadcast.249), dimensions={1}, to_apply=%all_to_all.41.reduce_sub_computation | reduce | bytes 3145732 | tf_op jit(solution)/shard_map/all_to_all | solution.py:35
  336.2 2.4 reshape.278
  342.4 16.6 %all_to_all.57 = bf16[16,2,12288]{2,1,0:T(2,128)(2,1)S(1)} all-to-all(bf16[16,2,12288]{2,1,0:T(2,128)(2,1)S(1)} %reshape.279), channel_id=1, replica_groups=mesh['row'=8,'col'=16,'samp'=2] {'col'}, dimensions={0} | all-to-all | bytes 1572864 | tf_op jit(solution)/shard_map/all_to_all | solution.py:20
  361.3 3.5 copy.144
  364.8 2.5 reshape.257
  370.1 4.4 convolution_bitcast_fusion.3
  374.5 2.6 pad_maximum_fusion
  377.1 2.4 reshape.258
  379.5 2.2 copy.171
  381.8 4.8 reshape.283
  386.6 5.4 all-to-all-start.7
  392.3 5.4 fusion.20
  397.7 28.6 %all-to-all-done.7 = f32[8,1,49152]{2,1,0:T(1,128)S(1)} async-done(((f32[8,1,49152]{2,1,0:T(1,128)}), f32[8,1,49152]{2,1,0:T(1,128)S(1)}, u32[]{:S(2)}, u32[]{:S(2)}) %all-to-all-start.7) | async-done | bytes 1572896 | tf_op jit(solution)/shard_map/all_to_all | solution.py:35
  426.3 6.3 %reduce.15 = f32[8,49152]{1,0:T(8,128)} reduce(f32[8,1,49152]{2,1,0:T(1,128)S(1)} %all-to-all-done.7, f32[]{:T(128)} %broadcast.249), dimensions={1}, to_apply=%all_to_all.48.reduce_sub_computation | reduce | bytes 3145732 | tf_op jit(solution)/shard_map/all_to_all | solution.py:35
  432.6 2.7 reshape.284
  437.9 1.6 fusion.42
  441.2 2.8 fusion.120
  444.0 14.9 %all_to_all.58 = f32[2,1,64,512]{3,2,1,0:T(8,128)S(1)} all-to-all(f32[2,1,64,512]{3,2,1,0:T(8,128)S(1)} %broadcast_in_dim.23), channel_id=1, replica_groups=mesh['row'=8,'col'=16,'samp'=2] {'samp'}, dimensions={0} | all-to-all | bytes 524288 | tf_op jit(solution)/shard_map/all_to_all | solution.py:20
  459.0 1.3 reduce.13
  460.6 11.2 %all_to_all.59 = f32[16,1,2048]{2,1,0:T(1,128)S(1)} all-to-all(f32[16,1,2048]{2,1,0:T(1,128)S(1)} %reshape.281), channel_id=1, replica_groups=mesh['row'=8,'col'=16,'samp'=2] {'col'}, dimensions={0} | all-to-all | bytes 262144 | tf_op jit(solution)/shard_map/all_to_all | solution.py:223
  473.4 2.0 fusion.45
  475.4 65.2 %all-gather.3.cloned.1.call-done = f32[2048,384]{1,0:T(8,128)} async-done(((f32[64,384]{1,0:T(8,128)}), f32[2048,384]{1,0:T(8,128)}) %all-gather.3.cloned.1.call-update) | async-done | bytes 3145744 | tf_op jit(solution)/shard_map/all_gather | solution.py:40
  540.6 2.2 reduce_sum.208
  (152 shorter events, 39.6 us)
Async XLA Ops:
  7.2 150.8 %copy-start = (bf16[768,3,48]{0,2,1:T(8,128)(2,1)S(1)}, bf16[768,3,48]{0,2,1:T(8,128)(2,1)}, u32[]{:S(2)}) copy-start(bf16[768,3,48]{0,2,1:T(8,128)(2,1)} %param.25) | copy-start | bytes 663556
  7.2 6.9 %copy-start.19 = (bf16[128,640]{1,0:T(8,128)(2,1)S(1)}, bf16[128,640]{1,0:T(8,128)(2,1)}, u32[]{:S(2)}) copy-start(bf16[128,640]{1,0:T(8,128)(2,1)} %param.19) | copy-start | bytes 491524
  15.1 2.4 copy-start.1
  20.2 96.8 %all-to-all-start = ((bf16[8,64,32,128]{3,2,1,0:T(8,128)(2,1)}), bf16[8,64,32,128]{3,2,1,0:T(8,128)(2,1)}, u32[]{:S(2)}, u32[]{:S(2)}) async-start(bf16[8,64,32,128]{3,2,1,0:T(8,128)(2,1)} %stack.4), calls=%async_computation | async-start | bytes 8388608 | tf_op jit(solution)/shard_map/all_to_all | solution.py:125
  26.4 246.5 %reduce-scatter.2.cloned.1.call-start = ((), (), s32[]{:S(2)}) async-start(), calls=%async_computation.9 | async-start | bytes 17825792 | tf_op jit(solution)/shard_map/reduce_scatter | solution.py:128
  152.6 0.8 copy-start.10
  152.6 1.2 copy-start.4
  153.5 2.8 copy-start.25
  154.3 3.6 copy-start.28
  154.4 3.6 copy-start.30
  156.4 0.8 copy-start.9
  158.7 0.7 copy-start.20
  159.7 10.3 %copy-start.17 = (bf16[48,768]{1,0:T(8,128)(2,1)S(1)}, bf16[48,768]{1,0:T(8,128)(2,1)}, u32[]{:S(2)}) copy-start(bf16[48,768]{1,0:T(8,128)(2,1)} %param.26) | copy-start | bytes 221188
  159.7 10.4 %copy-start.27 = (s32[512]{0:T(512)S(1)}, s32[512]{0:T(512)}, u32[]{:S(2)}) copy-start(s32[512]{0:T(512)} %param.17) | copy-start | bytes 6148
  161.7 25.7 %all-to-all-start.1 = ((bf16[8,2,24576]{2,1,0:T(2,128)(2,1)}), bf16[8,2,24576]{2,1,0:T(2,128)(2,1)}, u32[]{:S(2)}, u32[]{:S(2)}) async-start(bf16[8,2,24576]{2,1,0:T(2,128)(2,1)} %reshape.273), calls=%async_computation.2 | async-start | bytes 1572864 | tf_op jit(solution)/shard_map/all_to_all | solution.py:20
  273.0 1.7 copy-start.3
  274.6 1.3 copy-start.34
  276.0 2.7 copy-start.24
  277.8 0.8 copy-start.16
  280.5 12.5 %all-to-all-start.2 = ((bf16[16,2,1024]{2,1,0:T(2,128)(2,1)}), bf16[16,2,1024]{2,1,0:T(2,128)(2,1)S(1)}, u32[]{:S(2)}, u32[]{:S(2)}) async-start(bf16[16,2,1024]{2,1,0:T(2,128)(2,1)} %reshape.275), calls=%async_computation.3 | async-start | bytes 131072 | tf_op jit(solution)/shard_map/all_to_all | solution.py:145
  287.4 7.3 %copy-start.7 = (bf16[8,512,2,48]{1,3,0,2:T(8,128)(2,1)}, bf16[8,512,2,48]{1,3,0,2:T(8,128)(2,1)S(1)}, u32[]{:S(2)}) copy-start(bf16[8,512,2,48]{1,3,0,2:T(8,128)(2,1)S(1)} %reshape.252) | copy-start | bytes 2359300
  294.8 1.0 copy-start.13
  294.8 1.0 copy-start.32
  303.4 26.1 %all-to-all-start.3 = ((f32[16,1,24576]{2,1,0:T(1,128)}), f32[16,1,24576]{2,1,0:T(1,128)S(1)}, u32[]{:S(2)}, u32[]{:S(2)}) async-start(f32[16,1,24576]{2,1,0:T(1,128)} %reshape.277), calls=%async_computation.4 | async-start | bytes 3145728 | tf_op jit(solution)/shard_map/all_to_all | solution.py:35
  338.6 0.7 copy-start.22
  338.7 0.9 copy-start.23
  364.8 2.5 copy-start.18
  367.3 1.8 copy-start.14
  367.3 1.8 copy-start.33
  369.2 1.0 copy-start.11
  386.5 5.7 %copy-start.21 = (f32[64,48]{0,1:T(8,128)S(1)}, f32[64,48]{0,1:T(8,128)}, u32[]{:S(2)}) copy-start(f32[64,48]{0,1:T(8,128)} %get-tuple-element.11) | copy-start | bytes 36868
  386.5 5.7 %copy-start.8 = (bf16[8,512,2,48]{1,3,0,2:T(8,128)(2,1)S(1)}, bf16[8,512,2,48]{1,3,0,2:T(8,128)(2,1)}, u32[]{:S(2)}) copy-start(bf16[8,512,2,48]{1,3,0,2:T(8,128)(2,1)} %copy-done.7) | copy-start | bytes 2359300
  386.6 39.8 %all-to-all-start.7 = ((f32[8,1,49152]{2,1,0:T(1,128)}), f32[8,1,49152]{2,1,0:T(1,128)S(1)}, u32[]{:S(2)}, u32[]{:S(2)}) async-start(f32[8,1,49152]{2,1,0:T(1,128)} %reshape.283), calls=%async_computation.8 | async-start | bytes 3145728 | tf_op jit(solution)/shard_map/all_to_all | solution.py:35
  392.0 148.6 %all-gather.3.cloned.1.call-start = ((), (), s32[]{:S(2)}) async-start(), calls=%async_computation.10 | async-start | bytes 3244032 | tf_op jit(solution)/shard_map/all_gather | solution.py:40
  435.3 1.1 copy-start.5
  435.3 1.1 copy-start.31
  435.3 1.1 copy-start.35
  436.4 1.5 copy-start.6
  437.0 4.2 copy-start.12
  437.0 4.2 copy-start.15
  540.6 2.2 copy-start.26
  540.6 2.2 copy-start.29
  540.6 2.8 copy-start.2
Sparse Core Ops, SparseCore 0:
  152.8 120.1 reduce-scatter.1
  441.3 99.2 all-gather.2
